TPU v7x, 256 devices: a whole 4x4x8 slice. The times are simulated.
256 devices in a mesh: tm: 64 (over z, y, x_hi), chan: 4 (over x_lo, core).
Axes of the slice: x: 4 (x_hi: 2, x_lo: 2; x = x_hi * 2 + x_lo), y: 4, z: 8, core: 2. Of those that a mesh axis runs over, the one named last changes fastest.
Arguments:
- signal: bfloat16 [384, 8192], P('chan', 'tm'), may hold values from -6 to 6
- codes_init: float32 [128, 8192], P(None, 'tm'), may hold values from -2 to 2
- dictionary_init: float32 [128, 36864], P(None, 'chan'), may hold values from -6 to 6
- threshold: float32 [128], replicated, may hold values from 0.05 to 0.5
- plan: int32 [8], replicated, may hold values from 0 to 7, each once
Outputs:
- sparse_codes: float32 [128, 8192], P(None, 'tm')
- dictionary: float32 [128, 36864], P(None, 'chan')
- residual: float32 [384, 8192], P('chan', 'tm')
Inputs may be any that keep to these rules, and one draw needn't show every extreme that they name: `plan`: every atom block from 0 to 7 appears exactly once.
All inputs are finite; a program needn't handle non-finite values.
Results may differ from a plain program's by a relative error of at most 0.013.
Values may be sent and summed in bfloat16 or wider, within the bound.
A program may use at most 64 MiB of HBM per device.

v0:
```python
import jax
import jax.numpy as jnp
from jax import lax
from jax.sharding import PartitionSpec as P

C = 384
K = 128
L = 96
BLOCK_ATOMS = 16
INNER = 2
OUTER = 2
code_rate = 0.3
move_rate = 0.5
tiny_eps = 1e-06


def shifted(shard, axis, by):
    peers = lax.axis_size(axis)
    pairs = [(i, i + by) for i in range(peers) if 0 <= i + by < peers]
    return lax.ppermute(shard, axis, pairs)


def renew_atoms(old_atoms, across, mean_sq, spread):
    return (old_atoms + move_rate * across / jnp.sqrt(spread)[:, None]) / jnp.sqrt(mean_sq + 0.25)[
        :, None
    ]


def shards(signal, codes_init, dictionary_init, threshold, plan):
    segment = signal.shape[1]
    local_chan = signal.shape[0]
    unit_scale = (C * L) ** (-0.5)
    entries = C * L
    limit = threshold[:, None]

    def convolve(atom_cube, code_low):
        code_edge = shifted(code_low[:, segment - (L - 1) :], "tm", 1)
        extended = jnp.concatenate([code_edge, code_low], axis=1)
        lagged = jnp.stack(
            [extended[:, L - 1 - offset : L - 1 - offset + segment] for offset in range(L)], axis=1
        )
        return unit_scale * jnp.einsum(
            "kcl,klt->ct", atom_cube, lagged, preferred_element_type=jnp.float32
        )

    def resid_columns(resid_low):
        resid_edge = shifted(resid_low[:, : L - 1], "tm", -1)
        extended = jnp.concatenate([resid_low, resid_edge], axis=1)
        lagged = jnp.stack([extended[:, offset : offset + segment] for offset in range(L)], axis=1)
        return lagged.reshape(local_chan * L, segment)

    code_state = codes_init
    dictionary = dictionary_init
    residual = signal.astype(jnp.float32)
    for outer_step in range(OUTER):
        dict_low = dictionary.astype(jnp.bfloat16)
        atom_cube = dict_low.reshape(K, local_chan, L)
        for inner_step in range(INNER):
            code_low = code_state.astype(jnp.bfloat16)
            residual = signal.astype(jnp.float32) - convolve(atom_cube, code_low)
            lagged = resid_columns(residual.astype(jnp.bfloat16))
            partial_value = unit_scale * jnp.dot(
                dict_low, lagged, preferred_element_type=jnp.float32
            )
            scores = lax.psum(partial_value.astype(jnp.bfloat16), "chan").astype(jnp.float32)
            stepped = code_state + code_rate * scores
            code_state = stepped - jnp.clip(stepped, -limit, limit)
        code_low = code_state.astype(jnp.bfloat16)
        residual = signal.astype(jnp.float32) - convolve(atom_cube, code_low)
        lagged = resid_columns(residual.astype(jnp.bfloat16))
        first_row = plan[outer_step] * BLOCK_ATOMS
        code_block = lax.dynamic_slice_in_dim(code_low, first_row, BLOCK_ATOMS, 0)
        local_grad = lax.dot_general(
            code_block, lagged, (((1,), (1,)), ((), ())), preferred_element_type=jnp.float32
        )
        old_atoms = lax.dynamic_slice_in_dim(dictionary, first_row, BLOCK_ATOMS, 0)
        gradient = lax.psum(local_grad, "tm")
        dot_sum, square_sum = lax.psum(
            (jnp.sum(gradient * old_atoms, axis=1), jnp.sum(old_atoms * old_atoms, axis=1)), "chan"
        )
        mean_sq = square_sum / entries + tiny_eps
        along_coef = dot_sum / entries / mean_sq
        across = gradient - along_coef[:, None] * old_atoms
        spread = lax.psum(jnp.sum(across * across, axis=1), "chan") / entries + tiny_eps
        renewed = renew_atoms(old_atoms, across, mean_sq, spread)
        dictionary = lax.dynamic_update_slice_in_dim(dictionary, renewed, first_row, 0)
    return (code_state, dictionary, residual)


def solution(mesh):
    placed = (P("chan", "tm"), P(None, "tm"), P(None, "chan"), P(), P())
    return jax.shard_map(
        shards,
        mesh=mesh,
        in_specs=placed,
        out_specs=(P(None, "tm"), P(None, "chan"), P("chan", "tm")),
        check_vma=False,
    )
```

profile of v0, /device:TPU:1, one launch (start us, length us, event | category | flops | bytes accessed | tf_op | source)
XLA Modules:
  0.0 1790.4 jit_solution(17106135282890277592)
XLA Ops:
  7.2 5.0 copy.1188
  12.9 5.5 collective-permute-start
  18.4 3.6 copy.27
  87.9 3.6 constant_dynamic-update-slice_fusion.191
  91.5 1.3 collective-permute-start.1
  92.9 4.7 collective-permute-done.1
  163.2 2.6 copy.29
  166.6 11.6 psum.84
  178.2 5.0 collective-permute-start.2
  186.4 1.0 constant_dynamic-update-slice_fusion.383
  187.3 1.3 collective-permute-start.3
  188.6 5.1 collective-permute-done.3
  204.9 11.8 psum.85
  216.8 6.6 collective-permute-start.4
  226.7 1.6 constant_dynamic-update-slice_fusion.575
  228.4 1.5 collective-permute-start.5
  231.1 3.6 collective-permute-done.5
  300.3 2.6 copy.40
  302.9 1.6 fusion.1043
  304.6 640.8 %all-reduce.5.cloned.1.call-done = f32[16,9216]{1,0:T(8,128)} async-done(((f32[16,9216]{1,0:T(8,128)}), f32[16,9216]{1,0:T(8,128)}) %all-reduce.5.cloned.1.call-update) | async-done | bytes 589840 | tf_op jit(solution)/shard_map/psum | solution.py:77
  945.4 1.5 multiply_reduce_fusion.5
  946.9 36.4 %all-reduce.1 = (f32[16]{0:T(128)S(1)}, f32[16]{0:T(128)S(1)}) all-reduce(f32[16]{0:T(128)S(1)} %get-tuple-element.12, f32[16]{0:T(128)S(1)} %get-tuple-element.11), channel_id=1, replica_groups=mesh['tm'=64,'chan'=4] {'chan'}, use_global_device_ids=true, to_apply=%region_6.7 | all-reduce | flops 32 | bytes 256 | tf_op jit(solution)/shard_map/psum | solution.py:78
  983.3 1.5 multiply_reduce_fusion.3
  984.8 5.9 psum.89
  990.7 2.1 divide_dynamic-update-slice_fusion.1
  992.8 2.6 convert_element_type.92
  995.4 2.4 copy.41
  997.9 3.6 constant_dynamic-update-slice_fusion.671
  1001.5 1.7 collective-permute-start.6
  1003.2 4.4 collective-permute-done.6
  1017.8 1.1 fusion.32
  1018.9 11.4 psum.90
  1030.3 5.8 collective-permute-start.7
  1040.8 1.5 collective-permute-start.8
  1042.3 4.9 collective-permute-done.8
  1057.4 1.1 fusion.33
  1058.5 12.3 psum.91
  1070.9 6.0 collective-permute-start.9
  1080.6 1.6 constant_dynamic-update-slice_fusion.1055
  1082.2 1.5 collective-permute-start.10
  1084.4 4.2 collective-permute-done.10
  1098.8 1.6 fusion.1041
  1101.2 634.7 %all-reduce.7.cloned.1.call-done = f32[16,9216]{1,0:T(8,128)} async-done(((f32[16,9216]{1,0:T(8,128)}), f32[16,9216]{1,0:T(8,128)}) %all-reduce.7.cloned.1.call-update) | async-done | bytes 589840 | tf_op jit(solution)/shard_map/psum | solution.py:77
  1735.9 1.5 multiply_reduce_fusion.2
  1737.4 36.4 %all-reduce = (f32[16]{0:T(128)S(1)}, f32[16]{0:T(128)S(1)}) all-reduce(f32[16]{0:T(128)S(1)} %get-tuple-element.10, f32[16]{0:T(128)S(1)} %get-tuple-element.9), channel_id=1, replica_groups=mesh['tm'=64,'chan'=4] {'chan'}, use_global_device_ids=true, to_apply=%region_15.16 | all-reduce | flops 32 | bytes 256 | tf_op jit(solution)/shard_map/psum | solution.py:78
  1773.9 1.5 multiply_reduce_fusion
  1775.4 5.9 psum.95
  1781.3 2.1 divide_dynamic-update-slice_fusion
  (1099 shorter events, 254.4 us)
Async XLA Ops:
  7.2 5.0 copy-start.6
  7.2 938.2 %all-reduce.5.cloned.1.call-start = ((), (), s32[]{:S(2)}) async-start(), calls=%async_computation | async-start | bytes 1179648 | tf_op jit(solution)/shard_map/psum | solution.py:77
  12.9 9.1 collective-permute-start
  54.6 33.3 %copy-start.5 = (bf16[96,128]{1,0:T(8,128)(2,1)S(1)}, bf16[96,128]{1,0:T(8,128)(2,1)}, u32[]{:S(2)}) copy-start(bf16[96,128]{1,0:T(8,128)(2,1)} %param.5) | copy-start | bytes 73732
  87.9 5.0 copy-start.7
  91.5 6.1 collective-permute-start.1
  178.2 5.8 collective-permute-start.2
  187.3 6.4 collective-permute-start.3
  216.8 7.5 collective-permute-start.4
  226.7 1.7 copy-start.4
  226.7 3.2 copy-start.8
  228.4 6.3 collective-permute-start.5
  304.5 1431.4 %all-reduce.7.cloned.1.call-start = ((), (), s32[]{:S(2)}) async-start(), calls=%async_computation.1 | async-start | bytes 1179648 | tf_op jit(solution)/shard_map/psum | solution.py:77
  945.4 45.4 %copy-start.3 = (f32[16,9216]{1,0:T(8,128)S(1)}, f32[16,9216]{1,0:T(8,128)}, u32[]{:S(2)}) copy-start(f32[16,9216]{1,0:T(8,128)} %all-reduce.5.cloned.1.call-done) | copy-start | bytes 1769476
  1001.5 6.1 collective-permute-start.6
  1030.3 6.8 collective-permute-start.7
  1038.2 1.7 copy-start
  1040.8 6.4 collective-permute-start.8
  1070.9 7.0 collective-permute-start.9
  1079.0 1.7 copy-start.1
  1082.2 6.3 collective-permute-start.10
  1735.9 45.4 %copy-start.2 = (f32[16,9216]{1,0:T(8,128)S(1)}, f32[16,9216]{1,0:T(8,128)}, u32[]{:S(2)}) copy-start(f32[16,9216]{1,0:T(8,128)} %all-reduce.7.cloned.1.call-done) | copy-start | bytes 1769476
Sparse Core Ops, SparseCore 0:
  304.7 640.6 all-reduce.4
  1100.6 635.2 all-reduce.6
where the time goes:
time: 1800 us; the launch traced here: 1790 us
  waiting for transfers between devices  1310 us (73%)
  other arithmetic  255 us (14%)
  blocking collectives  132 us (7%)
  starting transfers between devices  37.7 us (2%)
  local copies, waits for them, and re-layouts  22.3 us (1%)
  matrix products  19.5 us (1%)
  between operations  18.7 us (1%)
    psum x2, waiting for transfers between devices, shards(): gradient = lax.psum(local_grad, 'tm')  1280 us
    unnamed x1039, other arithmetic  239 us
    psum x2, blocking collectives, shards(): lax.psum((jnp.sum(gradient * old_atoms, axis=1), jnp.sum(old_atoms * old_...  72.9 us
    psum x4, blocking collectives, shards(): lax.psum(partial_value.astype(jnp.bfloat16), 'chan').astype(jnp.float32)  47 us
    ppermute x11, starting transfers between devices, shifted(): return lax.ppermute(shard, axis, pairs)  37.6 us
  transfers between devices with their start and end apart: 13, of which 12 were waited for; matrix products, arithmetic and copies ran while one was open for 0% of the time, Pallas kernels for 0%

commit v1 on v0

--- a/solution.py
+++ b/solution.py
@@ -74,7 +74,8 @@
             code_block, lagged, (((1,), (1,)), ((), ())), preferred_element_type=jnp.float32
         )
         old_atoms = lax.dynamic_slice_in_dim(dictionary, first_row, BLOCK_ATOMS, 0)
-        gradient = lax.psum(local_grad, "tm")
+        terms = lax.all_gather(local_grad, "tm", axis=0, tiled=False)
+        gradient = terms.sum(axis=0)
         dot_sum, square_sum = lax.psum(
             (jnp.sum(gradient * old_atoms, axis=1), jnp.sum(old_atoms * old_atoms, axis=1)), "chan"
         )

time: 1800 us -> 1260 us (0.70)
  waiting for transfers between devices: 1310 us -> 801 us
  blocking collectives: 132 us -> 71.8 us
  other arithmetic: 255 us -> 280 us
    psum x2 -> x0, waiting for transfers between devices: 1280 us -> none  [shards(): gradient = lax.psum(local_grad, 'tm')]
    all_gather x0 -> x2, waiting for transfers between devices: none -> 771 us  [shards(): terms = lax.all_gather(local_grad, 'tm', axis=0, tiled=False)]
    psum x2, blocking collectives: 72.9 us -> 12.8 us  [shards(): lax.psum((jnp.sum(gradient * old_atoms, axis=1), jnp.sum(old_atoms * old_...]
    reduce_sum x0 -> x2, other arithmetic: none -> 26.3 us  [shards(): gradient = terms.sum(axis=0)]
where the time goes in v1:
time: 1260 us; the launch traced here: 1250 us
  waiting for transfers between devices  801 us (64%)
  other arithmetic  280 us (22%)
  blocking collectives  71.8 us (6%)
  starting transfers between devices  36 us (3%)
  local copies, waits for them, and re-layouts  22.2 us (2%)
  matrix products  19.5 us (2%)
  between operations  18.7 us (1%)
    all_gather x2, waiting for transfers between devices, shards(): terms = lax.all_gather(local_grad, 'tm', axis=0, tiled=False)  771 us
    unnamed x1039, other arithmetic  239 us
    psum x4, blocking collectives, shards(): lax.psum(partial_value.astype(jnp.bfloat16), 'chan').astype(jnp.float32)  47.1 us
    ppermute x11, starting transfers between devices, shifted(): return lax.ppermute(shard, axis, pairs)  36 us
    ppermute x11, waiting for transfers between devices, shifted(): return lax.ppermute(shard, axis, pairs)  30.3 us
    reduce_sum x2, other arithmetic, shards(): gradient = terms.sum(axis=0)  26.3 us
  transfers between devices with their start and end apart: 13, of which 12 were waited for; matrix products, arithmetic and copies ran while one was open for 0% of the time, Pallas kernels for 0%

profile of v1, /device:TPU:1, one launch (start us, length us, event | category | flops | bytes accessed | tf_op | source)
XLA Modules:
  0.0 1249.7 jit_solution(3248532126996530965)
XLA Ops:
  7.2 5.0 copy.1215
  12.9 5.5 collective-permute-start
  18.4 3.6 copy.56
  87.9 3.6 constant_dynamic-update-slice_fusion.191
  91.5 1.3 collective-permute-start.1
  92.9 4.7 collective-permute-done.1
  163.2 2.6 copy.58
  166.6 11.6 psum.70
  178.2 5.0 collective-permute-start.2
  187.3 1.3 collective-permute-start.3
  188.6 5.1 collective-permute-done.3
  204.9 11.8 psum.71
  216.8 6.6 collective-permute-start.4
  226.7 1.6 constant_dynamic-update-slice_fusion.575
  228.3 1.5 collective-permute-start.5
  231.1 3.6 collective-permute-done.5
  300.3 2.6 copy.69
  302.9 1.6 fusion.1043
  304.6 387.2 %all-gather.5.cloned.1.call-done = f32[1024,9216]{1,0:T(8,128)} async-done(((f32[16,9216]{1,0:T(8,128)}), f32[1024,9216]{1,0:T(8,128)}) %all-gather.5.cloned.1.call-update) | async-done | bytes 37748752 | tf_op jit(solution)/shard_map/all_gather | solution.py:77
  691.8 13.2 %reduce_sum.72 = f32[16,9216]{1,0:T(8,128)S(1)} reduce(f32[64,16,9216]{2,1,0:T(8,128)} %bitcast.4320, f32[]{:T(128)} %constant.26.clone.1), dimensions={0}, to_apply=%region_2.3 | reduce | flops 9289728 | bytes 38338564 | tf_op jit(solution)/shard_map/reduce_sum | solution.py:78
  705.0 1.3 multiply_reduce_fusion.5
  706.2 6.4 all-reduce.1
  712.7 1.3 multiply_reduce_fusion.3
  714.0 6.0 psum.74
  720.0 2.1 divide_dynamic-update-slice_fusion.1
  722.0 2.6 convert_element_type.92
  724.7 2.4 copy.70
  727.1 3.6 constant_dynamic-update-slice_fusion.671
  730.7 1.7 collective-permute-start.6
  732.4 4.4 collective-permute-done.6
  747.0 1.1 fusion.32
  748.1 11.4 psum.75
  759.6 4.2 collective-permute-start.7
  768.4 1.5 collective-permute-start.8
  769.9 4.9 collective-permute-done.8
  786.1 12.3 psum.76
  798.5 6.0 collective-permute-start.9
  808.2 1.6 constant_dynamic-update-slice_fusion.1055
  809.8 1.5 collective-permute-start.10
  812.0 4.2 collective-permute-done.10
  826.5 1.7 fusion.1041
  828.9 383.5 %all-gather.7.cloned.1.call-done = f32[1024,9216]{1,0:T(8,128)} async-done(((f32[16,9216]{1,0:T(8,128)}), f32[1024,9216]{1,0:T(8,128)}) %all-gather.7.cloned.1.call-update) | async-done | bytes 37748752 | tf_op jit(solution)/shard_map/all_gather | solution.py:77
  1212.4 13.2 %reduce_sum.76 = f32[16,9216]{1,0:T(8,128)S(1)} reduce(f32[64,16,9216]{2,1,0:T(8,128)} %bitcast.4319, f32[]{:T(128)} %constant.26.clone.1), dimensions={0}, to_apply=%region_11.12 | reduce | flops 9289728 | bytes 38338564 | tf_op jit(solution)/shard_map/reduce_sum | solution.py:78
  1225.6 1.3 multiply_reduce_fusion.2
  1226.8 6.4 all-reduce
  1233.3 1.3 multiply_reduce_fusion
  1234.6 6.0 psum.79
  1240.6 2.1 divide_dynamic-update-slice_fusion
  (1097 shorter events, 256.5 us)
Async XLA Ops:
  7.2 5.0 copy-start.4
  7.2 684.6 %all-gather.5.cloned.1.call-start = ((), (), s32[]{:S(2)}) async-start(), calls=%async_computation | async-start | bytes 38338560 | tf_op jit(solution)/shard_map/all_gather | solution.py:77
  12.9 9.1 collective-permute-start
  54.6 33.3 %copy-start.3 = (bf16[96,128]{1,0:T(8,128)(2,1)S(1)}, bf16[96,128]{1,0:T(8,128)(2,1)}, u32[]{:S(2)}) copy-start(bf16[96,128]{1,0:T(8,128)(2,1)} %param.5) | copy-start | bytes 73732
  87.9 5.0 copy-start.5
  91.5 6.1 collective-permute-start.1
  178.2 5.8 collective-permute-start.2
  187.3 6.4 collective-permute-start.3
  216.8 7.5 collective-permute-start.4
  226.7 1.6 copy-start.2
  226.7 3.1 copy-start.6
  228.3 6.3 collective-permute-start.5
  304.6 907.9 %all-gather.7.cloned.1.call-start = ((), (), s32[]{:S(2)}) async-start(), calls=%async_computation.1 | async-start | bytes 38338560 | tf_op jit(solution)/shard_map/all_gather | solution.py:77
  730.7 6.1 collective-permute-start.6
  759.6 5.1 collective-permute-start.7
  765.8 1.7 copy-start
  768.4 6.4 collective-permute-start.8
  798.5 7.0 collective-permute-start.9
  806.6 1.7 copy-start.1
  809.8 6.3 collective-permute-start.10
Sparse Core Ops, SparseCore 0:
  304.7 387.0 all-gather.4
  828.3 384.1 all-gather.6
